TPU v7x, 256 devices: a whole 4x4x8 slice. The times are simulated.
256 devices in a mesh: layer: 8 (over z_lo, y), cell: 32 (over z_hi, x, core).
Axes of the slice: x: 4, y: 4, z: 8 (z_hi: 4, z_lo: 2; z = z_hi * 2 + z_lo), core: 2. Of those that a mesh axis runs over, the one named last changes fastest.
Arguments:
- shower_state: float32 [2, 48, 1024], P(None, 'layer', 'cell'), may hold values from -6 to 6
- cell_valid: int32 [1024], replicated, may hold values 0 or 1
- layer_valid: int32 [48], replicated, may hold values 0 or 1
- energy_bin: int32 [2], replicated, may hold values from 0 to 63
- time_index: int32 [1], replicated, may hold values from 0 to 999
- embed_weight: float32 [512], replicated, may hold values from -6 to 6
- cell_embed: float32 [1024, 512], P('cell'), may hold values from -6 to 6
- layer_embed: float32 [48, 512], P('layer'), may hold values from -6 to 6
- energy_table: float32 [64, 512], replicated, may hold values from -6 to 6
- gain_cells: float32 [512], replicated, may hold values from 0.1 to 1.9
- cell_heads: bfloat16 [512, 1536], replicated, may hold values from -0.25 to 0.25
- cell_merge: bfloat16 [512, 512], replicated, may hold values from -0.25 to 0.25
- cell_scale: float32 [8], replicated, may hold values from 0.5 to 40
- gain_layers: float32 [512], replicated, may hold values from 0.1 to 1.9
- layer_heads: bfloat16 [512, 1536], replicated, may hold values from -0.25 to 0.25
- layer_merge: bfloat16 [512, 512], replicated, may hold values from -0.25 to 0.25
- layer_scale: float32 [8], replicated, may hold values from 0.5 to 40
- gain_expand: float32 [512], replicated, may hold values from 0.1 to 1.9
- expand_weight: bfloat16 [512, 2048], replicated, may hold values from -0.25 to 0.25
- reduce_weight: bfloat16 [2048, 512], replicated, may hold values from -0.125 to 0.125
- gain_final: float32 [512], replicated, may hold values from 0.1 to 1.9
- velocity_head: float32 [512], replicated, may hold values from -0.25 to 0.25
Outputs:
- velocity: float32 [2, 48, 1024], P(None, 'layer', 'cell')
- next_state: float32 [2, 48, 1024], P(None, 'layer', 'cell')
All inputs are finite; a program needn't handle non-finite values.
Results may differ from a plain program's by a relative error of at most 0.018.
The roundings to bfloat16 on the way count: a program that leaves them out, or rounds other values in their place, can miss the bound.
Values may be sent and summed in bfloat16 or wider, within the bound.
A program may use at most 192 MiB of HBM per device.

v0:
```python
import math
import jax
import jax.numpy as jnp
from jax import lax
from jax.sharding import PartitionSpec as P

D = 512
HEADS = 8
HDIM = 64
NBINS = 64
GRID = 1000
STEPS = 2
EPS = 1e-06


def normalize(hidden, gain):
    return hidden * lax.rsqrt(jnp.mean(hidden * hidden, -1, keepdims=True) + EPS) * gain


def head_norm(values):
    split = values.reshape(values.shape[:-1] + (HEADS, HDIM))
    return split * lax.rsqrt(jnp.mean(split * split, -1, keepdims=True) + EPS)


def split_heads(values):
    return values.reshape(values.shape[:-1] + (HEADS, HDIM)).astype(jnp.bfloat16)


def condition(energy_bin, time_index, energy_table):
    onehot = (jnp.arange(NBINS)[None, :] == energy_bin[:, None])[:, :, None]
    picked = jnp.sum(jnp.where(onehot, energy_table[None], 0.0), 1)
    moment = time_index[0].astype(jnp.float32) / GRID
    freqs = jnp.exp(-math.log(1000.0) * jnp.arange(D // 2).astype(jnp.float32) / (D // 2))
    angles = moment * 100.0 * freqs
    return picked + jnp.concatenate([jnp.sin(angles), jnp.cos(angles)])[None]


def online(carry, scores, allowed, values, form):
    top, total, accum = carry
    scores = jnp.where(allowed, scores, -1e30)
    new_top = jnp.maximum(top, jnp.max(scores, -1))
    weights = jnp.where(allowed, jnp.exp(scores - new_top[..., None]), 0.0)
    total = jnp.sum(weights, -1)
    accum = jnp.einsum(
        form, weights.astype(jnp.bfloat16), values, preferred_element_type=jnp.float32
    )
    return (new_top, total, accum)


def on_device(
    shower_state,
    cell_valid,
    layer_valid,
    energy_bin,
    time_index,
    embed_weight,
    cell_embed,
    layer_embed,
    energy_table,
    gain_cells,
    cell_heads,
    cell_merge,
    cell_scale,
    gain_layers,
    layer_heads,
    layer_merge,
    layer_scale,
    gain_expand,
    expand_weight,
    reduce_weight,
    gain_final,
    velocity_head,
):
    shw_count, lay_count, cell_count = shower_state.shape
    width = embed_weight.shape[0]
    cell_first = lax.axis_index("cell") * cell_count
    layer_first = lax.axis_index("layer") * lay_count
    cell_ok = lax.dynamic_slice_in_dim(cell_valid, cell_first, cell_count) == 1
    layer_ok = lax.dynamic_slice_in_dim(layer_valid, layer_first, lay_count) == 1
    cond = condition(energy_bin, time_index, energy_table)
    hidden = (
        shower_state[..., None] * embed_weight
        + cell_embed[None, None]
        + layer_embed[None, :, None]
        + cond[:, None, None]
    )
    normed = normalize(hidden, gain_cells).astype(jnp.bfloat16)
    query_ids = cell_first + jnp.arange(cell_count)
    cell_factor = cell_scale / math.sqrt(HDIM)
    start_cells = (
        jnp.full((shw_count, lay_count, HEADS, cell_count), -1e30, jnp.float32),
        jnp.zeros((shw_count, lay_count, HEADS, cell_count), jnp.float32),
        jnp.zeros((shw_count, lay_count, HEADS, cell_count, HDIM), jnp.float32),
    )
    queries = head_norm(
        jnp.dot(normed, cell_heads[:, :width], preferred_element_type=jnp.float32)
    ).astype(jnp.bfloat16)
    proj = jnp.dot(
        lax.all_gather(normed, "cell", axis=2, tiled=True),
        cell_heads[:, width:],
        preferred_element_type=jnp.float32,
    )
    keys = head_norm(proj[..., :width]).astype(jnp.bfloat16)
    values = split_heads(proj[..., width:])
    count = keys.shape[2]
    scores = (
        jnp.einsum("slqhd,slkhd->slhqk", queries, keys, preferred_element_type=jnp.float32)
        * cell_factor[None, None, :, None, None]
    )
    key_ok = cell_valid == 1
    allowed = key_ok[None, :] | (jnp.arange(count)[None, :] == query_ids[:, None])
    carry = online(start_cells, scores, allowed[None, None, None], values, "slhqk,slkhd->slhqd")
    result = carry[2] / carry[1][..., None]
    mixed = (
        jnp.transpose(result, (0, 1, 3, 2, 4))
        .reshape(shw_count, lay_count, cell_count, width)
        .astype(jnp.bfloat16)
    )
    hidden = hidden + jnp.dot(mixed, cell_merge, preferred_element_type=jnp.float32)
    normed = normalize(hidden, gain_layers).astype(jnp.bfloat16)
    layer_factor = layer_scale / math.sqrt(HDIM)
    proj = jnp.dot(normed, layer_heads, preferred_element_type=jnp.float32)
    layer_queries = head_norm(proj[..., :width]).astype(jnp.bfloat16)
    layer_keys = head_norm(proj[..., width : 2 * width]).astype(jnp.bfloat16)
    layer_values = split_heads(proj[..., 2 * width :])
    layer_ids = layer_first + jnp.arange(lay_count)
    start_layers = (
        jnp.full((shw_count, cell_count, HEADS, lay_count), -1e30, jnp.float32),
        jnp.zeros((shw_count, cell_count, HEADS, lay_count), jnp.float32),
        jnp.zeros((shw_count, cell_count, HEADS, lay_count, HDIM), jnp.float32),
    )
    pieces = (
        lax.all_gather(layer_keys, "layer", axis=1, tiled=True),
        lax.all_gather(layer_values, "layer", axis=1, tiled=True),
    )
    count = pieces[0].shape[1]
    scores = (
        jnp.einsum(
            "sqchd,skchd->schqk", layer_queries, pieces[0], preferred_element_type=jnp.float32
        )
        * layer_factor[None, None, :, None, None]
    )
    key_ok = layer_valid == 1
    allowed = key_ok[None, :] | (jnp.arange(count)[None, :] == layer_ids[:, None])
    carry = online(start_layers, scores, allowed[None, None, None], pieces[1], "schqk,skchd->schqd")
    result = carry[2] / carry[1][..., None]
    mixed = (
        jnp.transpose(result, (0, 3, 1, 2, 4))
        .reshape(shw_count, lay_count, cell_count, width)
        .astype(jnp.bfloat16)
    )
    hidden = hidden + jnp.dot(mixed, layer_merge, preferred_element_type=jnp.float32)
    normed = normalize(hidden, gain_expand).astype(jnp.bfloat16)
    inner = jax.nn.gelu(jnp.dot(normed, expand_weight, preferred_element_type=jnp.float32)).astype(
        jnp.bfloat16
    )
    hidden = hidden + jnp.dot(inner, reduce_weight, preferred_element_type=jnp.float32)
    velocity = jnp.sum(normalize(hidden, gain_final) * velocity_head, -1)
    velocity = (
        velocity
        * cell_ok[None, None, :].astype(jnp.float32)
        * layer_ok[None, :, None].astype(jnp.float32)
    )
    return (velocity, shower_state + velocity / STEPS)


def solution(mesh):
    return jax.shard_map(
        on_device,
        mesh=mesh,
        in_specs=(
            P(None, "layer", "cell"),
            P(),
            P(),
            P(),
            P(),
            P(),
            P("cell", None),
            P("layer", None),
            P(),
            P(),
            P(),
            P(),
            P(),
            P(),
            P(),
            P(),
            P(),
            P(),
            P(),
            P(),
            P(),
            P(),
        ),
        out_specs=(P(None, "layer", "cell"), P(None, "layer", "cell")),
        check_vma=False,
    )
```

profile of v0, /device:TPU:1, one launch (start us, length us, event | category | flops | bytes accessed | tf_op | source)
XLA Modules:
  0.0 406.8 jit_solution(17449303647220259367)
XLA Ops:
  11.7 1.9 multiply_convert_fusion.8
  13.7 1.6 fusion.57
  15.3 1.5 reshape.228
  16.7 1.9 multiply_reduce_fusion.3
  19.0 1.9 multiply_convert_fusion.3
  20.9 89.2 %all-gather.4.cloned.1.call-done = bf16[2,6,1024,512]{3,2,1,0:T(8,128)(2,1)} async-done(((bf16[2,6,32,512]{3,2,1,0:T(8,128)(2,1)}), bf16[2,6,1024,512]{3,2,1,0:T(8,128)(2,1)}) %all-gather.4.cloned.1.call-update) | async-done | bytes 12582928 | tf_op jit(solution)/shard_map/all_gather | solution.py:99
  110.2 24.7 %fusion.43 = f32[2,6,1024,1024]{2,3,1,0:T(8,128)} fusion(bf16[2,6,1024,512]{3,2,1,0:T(8,128)(2,1)} %all-gather.4.cloned.1.call-done, bf16[512,1536]{1,0:T(8,128)(2,1)} %param.32), kind=kOutput, calls=%fused_computation.53 | convolution fusion | flops 12884901888 | bytes 63963136 | tf_op jit(solution)/shard_map/dot_general | solution.py:98
  134.8 13.4 %slice.46 = bf16[2,6,1024,512]{2,3,1,0:T(8,128)(2,1)} slice(f32[2,6,1024,1024]{2,3,1,0:T(8,128)} %fusion.43), slice={[0:2], [0:6], [0:1024], [512:1024]} | slice | bytes 25165824 | tf_op jit(solution)/shard_map/slice | solution.py:104
  148.2 17.5 %slice.30 = f32[2,6,1024,512]{2,3,1,0:T(8,128)} slice(f32[2,6,1024,1024]{2,3,1,0:T(8,128)} %fusion.43), slice={[0:2], [0:6], [0:1024], [0:512]} | slice | bytes 50331648 | tf_op jit(solution)/shard_map/slice | solution.py:103
  165.8 10.2 %multiply_reduce_fusion = f32[2,6,1024,8]{2,3,1,0:T(8,128)S(1)} fusion(f32[2,6,1024,1024]{2,3,1,0:T(8,128)} %fusion.43), kind=kLoop, calls=%fused_computation.2 | loop fusion | flops 12484608 | bytes 25559040 | tf_op jit(solution)/shard_map/reduce_sum | solution.py:22
  176.0 16.4 %fusion.2 = (f32[2,6,8,32]{3,2,1,0:T(8,128)S(1)}, f32[2,6,8,32,1024]{4,3,2,1,0:T(8,128)}) fusion(f32[8]{0:T(128)S(1)} %broadcast_multiply_fusion.1, pred[32,1024]{1,0:T(8,128)(4,1)S(1)} %fusion.66, f32[2,6,1024,8,64]{2,4,3,1,0:T(8,128)} %bitcast.78, f32[2,6,1024,8]{2,3,1,0:T(8,128)S(1)} %add_rsqrt_fusion, ...), kind=kOutput, calls=%fused_computation.7 | convolution fusion | flops 424670208 | bytes 38580256 | tf_op jit(solution)/shard_map/slqhd,slkhd->slhqk/dot_general | solution.py:107
  192.4 6.8 %fusion.3 = f32[2,6,8,32]{3,2,1,0:T(8,128)S(1)} fusion(f32[2,6,8,32,1024]{4,3,2,1,0:T(8,128)} %get-tuple-element.13, f32[2,6,8,32]{3,2,1,0:T(8,128)S(1)} %broadcast_maximum_fusion.1, f32[8]{0:T(128)S(1)} %broadcast_multiply_fusion.1, pred[32,1024]{1,0:T(8,128)(4,1)S(1)} %fusion.66), kind=kLoop, calls=%fused_computation.8 | loop fusion | flops 15725568 | bytes 12640288 | tf_op jit(solution)/shard_map/reduce_sum | solution.py:43
  199.2 14.3 %fusion.33 = bf16[2,6,32,8,64]{4,2,3,1,0:T(8,128)(2,1)} fusion(bf16[2,6,1024,8,64]{2,4,3,1,0:T(8,128)(2,1)} %bitcast.79, f32[2,6,8,32,1024]{4,3,2,1,0:T(8,128)} %get-tuple-element.13, f32[2,6,8,32]{3,2,1,0:T(8,128)S(1)} %broadcast_maximum_fusion.1, f32[8]{0:T(128)S(1)} %broadcast_multiply_fusion.1, pred[32,1024]{1,0:T(8,128)(4,1)S(1)} %fusion.66, ...), kind=kOutput, calls=%fused_computation.40 | convolution fusion | flops 418775040 | bytes 25616416 | tf_op jit(solution)/shard_map/slhqk,slkhd->slhqd/dot_general | solution.py:44
  213.6 1.5 copy.73
  215.5 1.6 multiply_reduce_fusion.7
  218.0 1.4 copy-done.2
  220.5 1.5 reshape.231
  221.9 1.9 multiply_reduce_fusion.1
  224.1 2.8 fusion.34
  227.0 1.2 slice.47
  229.8 2.6 reshape.230
  232.4 1.9 multiply_reduce_fusion.2
  234.5 1.9 multiply_convert_fusion.2
  236.4 70.1 %all-gather.6.cloned.1.call-done = bf16[2,48,32,8,64]{4,3,2,0,1:T(8,128)(2,1)} async-done(((bf16[2,6,32,8,64]{4,3,2,0,1:T(8,128)(2,1)}), bf16[2,48,32,8,64]{4,3,2,0,1:T(8,128)(2,1)}) %all-gather.6.cloned.1.call-update) | async-done | bytes 3145744 | tf_op jit(solution)/shard_map/all_gather | solution.py:133
  306.5 8.8 %fusion.28 = (f32[2,32,8,6]{3,2,1,0:T(8,128)S(1)}, f32[2,32,8,6,48]{4,3,2,1,0:T(8,128)S(1)}) fusion(f32[8]{0:T(128)S(1)} %broadcast_multiply_fusion, pred[6,48]{1,0:T(8,128)(4,1)S(1)} %fusion.67, bf16[2,48,32,8,64]{4,3,2,0,1:T(8,128)(2,1)} %all-gather.6.cloned.1.call-done, bf16[2,6,32,8,64]{4,3,2,1,0:T(8,128)(2,1)S(1)} %multiply_convert_fusion.2), kind=kOutput, calls=%fused_computation.36 | convolution fusion | flops 19313664 | bytes 4141376 | tf_op jit(solution)/shard_map/sqchd,skchd->schqk/dot_general | solution.py:138
  315.3 1.3 copy-done.1
  316.6 1.5 fusion.37
  318.2 63.8 %all-gather.8.cloned.1.call-done = bf16[2,48,32,8,64]{4,3,2,0,1:T(8,128)(2,1)} async-done(((bf16[2,6,32,8,64]{4,3,2,0,1:T(8,128)(2,1)}), bf16[2,48,32,8,64]{4,3,2,0,1:T(8,128)(2,1)}) %all-gather.8.cloned.1.call-update) | async-done | bytes 3145744 | tf_op jit(solution)/shard_map/all_gather | solution.py:134
  382.0 8.7 %fusion.27 = bf16[2,6,32,8,64]{4,1,3,2,0:T(8,128)(2,1)S(1)} fusion(bf16[2,48,32,8,64]{4,3,2,0,1:T(8,128)(2,1)} %all-gather.8.cloned.1.call-done, f32[2,32,8,6,48]{4,3,2,1,0:T(8,128)} %copy-done.1, f32[2,6,32,8]{1,3,2,0:T(8,128)S(1)} %bitcast.80, f32[2,32,8,6]{3,2,1,0:T(8,128)S(1)} %broadcast_maximum_fusion, f32[8]{0:T(128)S(1)} %broadcast_multiply_fusion, ...), kind=kOutput, calls=%fused_computation.33 | convolution fusion | flops 20004864 | bytes 4153664 | tf_op jit(solution)/shard_map/schqk,skchd->schqd/dot_general | solution.py:44
  391.2 1.7 multiply_reduce_fusion.6
  393.1 4.5 %multiply_reduce_fusion.5 = (f32[2,6,32]{2,1,0:T(8,128)S(1)}, f32[2,6,32,512]{3,2,1,0:T(8,128)}) fusion(f32[2,6,32,512]{3,2,1,0:T(8,128)S(1)} %get-tuple-element.19, bf16[2048,512]{1,0:T(8,128)(2,1)S(1)} %copy-done, bf16[512,2048]{1,0:T(8,128)(2,1)} %param.40, f32[512]{0:T(512)S(1)} %copy-done.13, f32[2,6,32]{2,1,0:T(8,128)S(1)} %add_rsqrt_fusion.5), kind=kOutput, calls=%fused_computation.65 | convolution fusion | flops 1618869888 | bytes 5772288 | tf_op jit(solution)/shard_map/dot_general | solution.py:157
  397.6 1.4 multiply_reduce_fusion.4
  (81 shorter events, 10.7 us)
Async XLA Ops:
  7.2 385.8 %copy-start = (bf16[2048,512]{1,0:T(8,128)(2,1)S(1)}, bf16[2048,512]{1,0:T(8,128)(2,1)}, u32[]{:S(2)}) copy-start(bf16[2048,512]{1,0:T(8,128)(2,1)} %param.41) | copy-start | bytes 6291460
  7.2 103.0 %all-gather.4.cloned.1.call-start = ((), (), s32[]{:S(2)}) async-start(), calls=%async_computation | async-start | bytes 12976128 | tf_op jit(solution)/shard_map/all_gather | solution.py:99
  13.6 292.9 %all-gather.6.cloned.1.call-start = ((), (), s32[]{:S(2)}) async-start(), calls=%async_computation.1 | async-start | bytes 7077888 | tf_op jit(solution)/shard_map/all_gather | solution.py:133
  13.6 5.3 %copy-start.14 = (f32[8]{0:T(128)S(1)}, f32[8]{0:T(128)}, u32[]{:S(2)}) copy-start(f32[8]{0:T(128)} %param.34) | copy-start | bytes 100
  13.7 5.3 %copy-start.10 = (s32[1024]{0:T(1024)S(1)}, s32[1024]{0:T(1024)}, u32[]{:S(2)}) copy-start(s32[1024]{0:T(1024)} %param.23) | copy-start | bytes 12292
  199.2 16.3 %copy-start.5 = (f32[32,512]{1,0:T(8,128)S(1)}, f32[32,512]{1,0:T(8,128)}, u32[]{:S(2)}) copy-start(f32[32,512]{1,0:T(8,128)} %param.28) | copy-start | bytes 196612
  199.2 16.3 %copy-start.6 = (f32[6,512]{1,0:T(8,128)S(1)}, f32[6,512]{1,0:T(8,128)}, u32[]{:S(2)}) copy-start(f32[6,512]{1,0:T(8,128)} %param.29) | copy-start | bytes 36868
  199.2 16.3 %copy-start.8 = (f32[512]{0:T(512)S(1)}, f32[512]{0:T(512)}, u32[]{:S(2)}) copy-start(f32[512]{0:T(512)} %param.27) | copy-start | bytes 6148
  213.6 3.6 copy-start.9
  215.5 1.7 copy-start.4
  217.2 3.3 copy-start.3
  218.0 1.4 copy-start.2
  226.9 2.8 copy-start.15
  226.9 2.8 copy-start.16
  226.9 155.0 %all-gather.8.cloned.1.call-start = ((), (), s32[]{:S(2)}) async-start(), calls=%async_computation.2 | async-start | bytes 7077888 | tf_op jit(solution)/shard_map/all_gather | solution.py:134
  315.3 1.4 copy-start.1
  390.6 2.4 copy-start.13
  393.0 4.6 %copy-start.11 = (f32[512]{0:T(512)S(1)}, f32[512]{0:T(512)}, u32[]{:S(2)}) copy-start(f32[512]{0:T(512)} %param.43) | copy-start | bytes 6148
  393.0 4.6 %copy-start.12 = (f32[512]{0:T(512)S(1)}, f32[512]{0:T(512)}, u32[]{:S(2)}) copy-start(f32[512]{0:T(512)} %param.42) | copy-start | bytes 6148
  393.0 6.0 %copy-start.7 = (f32[2,6,32]{2,0,1:T(2,128)S(1)}, f32[2,6,32]{2,0,1:T(2,128)}, u32[]{:S(2)}) copy-start(f32[2,6,32]{2,0,1:T(2,128)} %param.22) | copy-start | bytes 4612
Sparse Core Ops, SparseCore 0:
  13.7 96.4 all-gather.3
  227.0 79.4 all-gather.5
  308.3 73.6 all-gather.7
where the time goes:
time: 408 us; the launch traced here: 407 us
  waiting for transfers between devices  223 us (55%)
  matrix products  83.2 us (20%)
  local copies, waits for them, and re-layouts  47.8 us (12%)
  other arithmetic  37.7 us (9%)
  between operations  14.9 us (4%)
    all_gather x1, waiting for transfers between devices, on_device(): lax.all_gather(normed, 'cell', axis=2, tiled=True)  89.2 us
    all_gather x1, waiting for transfers between devices, on_device(): lax.all_gather(layer_keys, 'layer', axis=1, tiled=True)  70.1 us
    all_gather x1, waiting for transfers between devices, on_device(): lax.all_gather(layer_values, 'layer', axis=1, tiled=True)  63.8 us
    dot_general x1, matrix products, on_device(): jnp.dot(lax.all_gather(normed, 'cell', axis=2, tiled=True), cell_heads[:,...  24.7 us
    dot_general x2, matrix products, online(): jnp.einsum(form, weights.astype(jnp.bfloat16), values, preferred_element_...  23 us
    slice x1, local copies, waits for them, and re-layouts, on_device(): keys = head_norm(proj[..., :width]).astype(jnp.bfloat16)  17.5 us
    dot_general x1, matrix products, on_device(): jnp.einsum('slqhd,slkhd->slhqk', queries, keys, preferred_element_type=jn...  16.4 us
    reduce_sum x4, other arithmetic, head_norm(): return split * lax.rsqrt(jnp.mean(split * split, -1, keepdims=True) + EPS)  15.9 us
  transfers between devices with their start and end apart: 3, of which 3 were waited for; matrix products, arithmetic and copies ran while one was open for 7% of the time, Pallas kernels for 0%

commit v1 on v0

--- a/solution.py
+++ b/solution.py
@@ -131,7 +131,10 @@
     )
     pieces = (
         lax.all_gather(layer_keys, "layer", axis=1, tiled=True),
-        lax.all_gather(layer_values, "layer", axis=1, tiled=True),
+        jnp.concatenate(
+            lax.all_to_all(jnp.stack([layer_values] * lax.axis_size("layer")), "layer", 0, 0),
+            axis=1,
+        ),
     )
     count = pieces[0].shape[1]
     scores = (

time: 408 us -> 381 us (0.934)
  waiting for transfers between devices: 223 us -> 161 us
  local copies, waits for them, and re-layouts: 47.8 us -> 70.6 us
  starting transfers between devices: 0.12 us -> 10.8 us
    all_gather x1 -> x0, waiting for transfers between devices: 63.8 us -> none  [on_device(): lax.all_gather(layer_values, 'layer', axis=1, tiled=True)]
    all_to_all x0 -> x1, waiting for transfers between devices: none -> 40.7 us  [on_device(): lax.all_to_all(jnp.stack([layer_values] * lax.axis_size('layer')), 'layer...]
    all_gather x1, waiting for transfers between devices: 70.1 us -> 30.5 us  [on_device(): lax.all_gather(layer_keys, 'layer', axis=1, tiled=True)]
    unnamed x37 -> x41, local copies, waits for them, and re-layouts: 4.71 us -> 19.8 us
    all_to_all x0 -> x1, starting transfers between devices: none -> 10.7 us  [on_device(): lax.all_to_all(jnp.stack([layer_values] * lax.axis_size('layer')), 'layer...]
    all_to_all x0 -> x1, local copies, waits for them, and re-layouts: none -> 6.3 us  [on_device(): lax.all_to_all(jnp.stack([layer_values] * lax.axis_size('layer')), 'layer...]
    another operation x0 -> x1, local copies, waits for them, and re-layouts: none -> 4.21 us  [on_device(): jnp.stack([layer_values] * lax.axis_size('layer'))]
  transfers between devices with their start and end apart: 3 -> 3, of which waited for: 3 -> 3; matrix products, arithmetic and copies ran while one was open for 7% -> 9% of each run, Pallas kernels for 0% -> 0%
where the time goes in v1:
time: 381 us; the launch traced here: 380 us
  waiting for transfers between devices  161 us (42%)
  matrix products  85.4 us (22%)
  local copies, waits for them, and re-layouts  70.6 us (19%)
  other arithmetic  37.5 us (10%)
  between operations  15.2 us (4%)
  starting transfers between devices  10.8 us (3%)
    all_gather x1, waiting for transfers between devices, on_device(): lax.all_gather(normed, 'cell', axis=2, tiled=True)  89.3 us
    all_to_all x1, waiting for transfers between devices, on_device(): lax.all_to_all(jnp.stack([layer_values] * lax.axis_size('layer')), 'layer...  40.7 us
    all_gather x1, waiting for transfers between devices, on_device(): lax.all_gather(layer_keys, 'layer', axis=1, tiled=True)  30.5 us
    dot_general x2, matrix products, online(): jnp.einsum(form, weights.astype(jnp.bfloat16), values, preferred_element_...  25.1 us
    dot_general x1, matrix products, on_device(): jnp.dot(lax.all_gather(normed, 'cell', axis=2, tiled=True), cell_heads[:,...  24.7 us
    unnamed x41, local copies, waits for them, and re-layouts  19.8 us
    slice x1, local copies, waits for them, and re-layouts, on_device(): keys = head_norm(proj[..., :width]).astype(jnp.bfloat16)  17.5 us
    dot_general x1, matrix products, on_device(): jnp.einsum('slqhd,slkhd->slhqk', queries, keys, preferred_element_type=jn...  16.4 us
  transfers between devices with their start and end apart: 3, of which 3 were waited for; matrix products, arithmetic and copies ran while one was open for 9% of the time, Pallas kernels for 0%

profile of v1, /device:TPU:1, one launch (start us, length us, event | category | flops | bytes accessed | tf_op | source)
XLA Modules:
  0.0 380.0 jit_solution(28393359245512313)
XLA Ops:
  11.7 1.9 multiply_convert_fusion.8
  13.6 1.6 fusion.57
  15.2 1.5 reshape.237
  16.7 1.9 multiply_reduce_fusion.3
  19.0 1.9 multiply_convert_fusion.3
  20.9 89.3 %all-gather.3.cloned.1.call-done = bf16[2,6,1024,512]{3,2,1,0:T(8,128)(2,1)} async-done(((bf16[2,6,32,512]{3,2,1,0:T(8,128)(2,1)}), bf16[2,6,1024,512]{3,2,1,0:T(8,128)(2,1)}) %all-gather.3.cloned.1.call-update) | async-done | bytes 12582928 | tf_op jit(solution)/shard_map/all_gather | solution.py:99
  110.2 24.7 %fusion.43 = f32[2,6,1024,1024]{2,3,1,0:T(8,128)} fusion(bf16[2,6,1024,512]{3,2,1,0:T(8,128)(2,1)} %all-gather.3.cloned.1.call-done, bf16[512,1536]{1,0:T(8,128)(2,1)} %param.32), kind=kOutput, calls=%fused_computation.53 | convolution fusion | flops 12884901888 | bytes 63963136 | tf_op jit(solution)/shard_map/dot_general | solution.py:98
  134.8 13.4 %slice.46 = bf16[2,6,1024,512]{2,3,1,0:T(8,128)(2,1)} slice(f32[2,6,1024,1024]{2,3,1,0:T(8,128)} %fusion.43), slice={[0:2], [0:6], [0:1024], [512:1024]} | slice | bytes 25165824 | tf_op jit(solution)/shard_map/slice | solution.py:104
  148.2 17.5 %slice.30 = f32[2,6,1024,512]{2,3,1,0:T(8,128)} slice(f32[2,6,1024,1024]{2,3,1,0:T(8,128)} %fusion.43), slice={[0:2], [0:6], [0:1024], [0:512]} | slice | bytes 50331648 | tf_op jit(solution)/shard_map/slice | solution.py:103
  165.8 10.2 %multiply_reduce_fusion = f32[2,6,1024,8]{2,3,1,0:T(8,128)S(1)} fusion(f32[2,6,1024,1024]{2,3,1,0:T(8,128)} %fusion.43), kind=kLoop, calls=%fused_computation.2 | loop fusion | flops 12484608 | bytes 25559040 | tf_op jit(solution)/shard_map/reduce_sum | solution.py:22
  176.1 16.4 %fusion.2 = (f32[2,6,8,32]{3,2,1,0:T(8,128)S(1)}, f32[2,6,8,32,1024]{4,3,2,1,0:T(8,128)}) fusion(f32[8]{0:T(128)S(1)} %broadcast_multiply_fusion.1, pred[32,1024]{1,0:T(8,128)(4,1)S(1)} %fusion.66, f32[2,6,1024,8,64]{2,4,3,1,0:T(8,128)} %bitcast.81, f32[2,6,1024,8]{2,3,1,0:T(8,128)S(1)} %add_rsqrt_fusion, ...), kind=kOutput, calls=%fused_computation.7 | convolution fusion | flops 424670208 | bytes 38580256 | tf_op jit(solution)/shard_map/slqhd,slkhd->slhqk/dot_general | solution.py:107
  192.4 6.8 %fusion.3 = f32[2,6,8,32]{3,2,1,0:T(8,128)S(1)} fusion(f32[2,6,8,32,1024]{4,3,2,1,0:T(8,128)} %get-tuple-element.13, f32[2,6,8,32]{3,2,1,0:T(8,128)S(1)} %broadcast_maximum_fusion.1, f32[8]{0:T(128)S(1)} %broadcast_multiply_fusion.1, pred[32,1024]{1,0:T(8,128)(4,1)S(1)} %fusion.66), kind=kLoop, calls=%fused_computation.8 | loop fusion | flops 15725568 | bytes 12640288 | tf_op jit(solution)/shard_map/reduce_sum | solution.py:43
  199.2 14.4 %fusion.33 = bf16[2,6,32,8,64]{4,2,3,1,0:T(8,128)(2,1)} fusion(bf16[2,6,1024,8,64]{2,4,3,1,0:T(8,128)(2,1)} %bitcast.82, f32[2,6,8,32,1024]{4,3,2,1,0:T(8,128)} %get-tuple-element.13, f32[2,6,8,32]{3,2,1,0:T(8,128)S(1)} %broadcast_maximum_fusion.1, f32[8]{0:T(128)S(1)} %broadcast_multiply_fusion.1, pred[32,1024]{1,0:T(8,128)(4,1)S(1)} %fusion.66, ...), kind=kOutput, calls=%fused_computation.40 | convolution fusion | flops 418775040 | bytes 25616416 | tf_op jit(solution)/shard_map/slhqk,slkhd->slhqd/dot_general | solution.py:44
  213.6 1.5 copy.73
  215.6 1.6 multiply_reduce_fusion.7
  219.9 4.2 %stack.2 = bf16[8,2,6,32,8,64]{5,4,3,2,1,0:T(8,128)(2,1)} broadcast(bf16[2,6,32,8,64]{4,3,2,1,0:T(8,128)(2,1)S(1)} %convert_element_type.80), dimensions={1,2,3,4,5} | broadcast | bytes 3538944 | tf_op jit(solution)/shard_map/stack | solution.py:135
  224.1 8.9 %reshape.250 = bf16[8,2,98304]{2,1,0:T(2,128)(2,1)} reshape(bf16[8,2,6,32,8,64]{5,4,3,2,1,0:T(8,128)(2,1)} %stack.2) | data formatting | bytes 6291456
  233.0 10.7 %all-to-all-start = ((bf16[8,2,98304]{2,1,0:T(2,128)(2,1)}), bf16[8,2,98304]{2,1,0:T(2,128)(2,1)}, u32[]{:S(2)}, u32[]{:S(2)}) async-start(bf16[8,2,98304]{2,1,0:T(2,128)(2,1)} %reshape.250), calls=%async_computation | async-start | bytes 6291456 | tf_op jit(solution)/shard_map/all_to_all | solution.py:135
  243.8 1.5 reshape.240
  245.3 2.0 multiply_reduce_fusion.1
  247.5 2.8 fusion.34
  250.6 1.5 reshape.239
  252.1 1.9 multiply_reduce_fusion.2
  254.2 1.9 multiply_convert_fusion.2
  256.1 40.7 %all-to-all-done = bf16[8,2,98304]{2,1,0:T(2,128)(2,1)} async-done(((bf16[8,2,98304]{2,1,0:T(2,128)(2,1)}), bf16[8,2,98304]{2,1,0:T(2,128)(2,1)}, u32[]{:S(2)}, u32[]{:S(2)}) %all-to-all-start) | async-done | bytes 3145760 | tf_op jit(solution)/shard_map/all_to_all | solution.py:135
  296.9 8.8 %reshape.251 = bf16[8,2,6,32,8,64]{5,4,3,2,1,0:T(8,128)(2,1)} reshape(bf16[8,2,98304]{2,1,0:T(2,128)(2,1)} %all-to-all-done) | data formatting | bytes 6291456
  305.7 6.3 %copy.81 = bf16[8,2,6,32,8,64]{5,4,3,2,0,1:T(8,128)(2,1)} copy(bf16[8,2,6,32,8,64]{5,4,3,2,1,0:T(8,128)(2,1)} %reshape.251) | data formatting | bytes 6291456 | tf_op jit(solution)/shard_map/all_to_all | solution.py:135
  312.0 30.5 %all-gather.5.cloned.1.call-done = bf16[2,48,32,8,64]{4,3,2,0,1:T(8,128)(2,1)} async-done(((bf16[2,6,32,8,64]{4,3,2,0,1:T(8,128)(2,1)}), bf16[2,48,32,8,64]{4,3,2,0,1:T(8,128)(2,1)}) %all-gather.5.cloned.1.call-update) | async-done | bytes 3145744 | tf_op jit(solution)/shard_map/all_gather | solution.py:133
  342.5 8.9 %fusion.28 = (f32[2,32,8,6]{3,2,1,0:T(8,128)S(1)}, f32[2,32,8,6,48]{4,3,2,1,0:T(8,128)S(1)}) fusion(f32[8]{0:T(128)S(1)} %broadcast_multiply_fusion, pred[6,48]{1,0:T(8,128)(4,1)S(1)} %fusion.67, bf16[2,48,32,8,64]{4,3,2,0,1:T(8,128)(2,1)} %all-gather.5.cloned.1.call-done, bf16[2,6,32,8,64]{4,3,2,1,0:T(8,128)(2,1)S(1)} %multiply_convert_fusion.2), kind=kOutput, calls=%fused_computation.36 | convolution fusion | flops 19313664 | bytes 4141376 | tf_op jit(solution)/shard_map/sqchd,skchd->schqk/dot_general | solution.py:141
  352.8 10.8 %fusion.27 = bf16[2,6,32,8,64]{4,1,3,2,0:T(8,128)(2,1)S(1)} fusion(bf16[2,48,32,8,64]{4,3,2,1,0:T(8,128)(2,1)S(1)} %bitcast.83, f32[2,32,8,6,48]{4,3,2,1,0:T(8,128)S(1)} %get-tuple-element.17, f32[2,6,32,8]{1,3,2,0:T(8,128)S(1)} %bitcast.84, f32[2,32,8,6]{3,2,1,0:T(8,128)S(1)} %broadcast_maximum_fusion, f32[8]{0:T(128)S(1)} %broadcast_multiply_fusion, ...), kind=kOutput, calls=%fused_computation.33 | convolution fusion | flops 20004864 | bytes 4153664 | tf_op jit(solution)/shard_map/schqk,skchd->schqd/dot_general | solution.py:44
  364.1 1.7 multiply_reduce_fusion.6
  366.0 4.5 %multiply_reduce_fusion.5 = (f32[2,6,32]{2,1,0:T(8,128)S(1)}, f32[2,6,32,512]{3,2,1,0:T(8,128)}) fusion(f32[2,6,32,512]{3,2,1,0:T(8,128)S(1)} %get-tuple-element.19, bf16[2048,512]{1,0:T(8,128)(2,1)S(1)} %copy-done, bf16[512,2048]{1,0:T(8,128)(2,1)} %param.40, f32[512]{0:T(512)S(1)} %copy-done.14, f32[2,6,32]{2,1,0:T(8,128)S(1)} %add_rsqrt_fusion.5), kind=kOutput, calls=%fused_computation.65 | convolution fusion | flops 1618869888 | bytes 5772288 | tf_op jit(solution)/shard_map/dot_general | solution.py:160
  (85 shorter events, 12.8 us)
Async XLA Ops:
  7.2 358.7 %copy-start = (bf16[2048,512]{1,0:T(8,128)(2,1)S(1)}, bf16[2048,512]{1,0:T(8,128)(2,1)}, u32[]{:S(2)}) copy-start(bf16[2048,512]{1,0:T(8,128)(2,1)} %param.41) | copy-start | bytes 6291460
  7.2 103.0 %all-gather.3.cloned.1.call-start = ((), (), s32[]{:S(2)}) async-start(), calls=%async_computation.1 | async-start | bytes 12976128 | tf_op jit(solution)/shard_map/all_gather | solution.py:99
  13.6 5.3 %copy-start.15 = (f32[8]{0:T(128)S(1)}, f32[8]{0:T(128)}, u32[]{:S(2)}) copy-start(f32[8]{0:T(128)} %param.34) | copy-start | bytes 100
  13.6 5.3 %copy-start.11 = (s32[1024]{0:T(1024)S(1)}, s32[1024]{0:T(1024)}, u32[]{:S(2)}) copy-start(s32[1024]{0:T(1024)} %param.23) | copy-start | bytes 12292
  199.2 16.3 %copy-start.6 = (f32[32,512]{1,0:T(8,128)S(1)}, f32[32,512]{1,0:T(8,128)}, u32[]{:S(2)}) copy-start(f32[32,512]{1,0:T(8,128)} %param.28) | copy-start | bytes 196612
  199.2 16.3 %copy-start.7 = (f32[6,512]{1,0:T(8,128)S(1)}, f32[6,512]{1,0:T(8,128)}, u32[]{:S(2)}) copy-start(f32[6,512]{1,0:T(8,128)} %param.29) | copy-start | bytes 36868
  199.2 16.3 %copy-start.9 = (f32[512]{0:T(512)S(1)}, f32[512]{0:T(512)}, u32[]{:S(2)}) copy-start(f32[512]{0:T(512)} %param.27) | copy-start | bytes 6148
  213.6 3.6 copy-start.10
  215.6 1.7 copy-start.5
  217.2 0.9 copy-start.2
  233.0 10.8 %copy-start.4 = (f32[2,6,32,512]{3,2,1,0:T(8,128)S(1)}, f32[2,6,32,512]{3,2,1,0:T(8,128)}, u32[]{:S(2)}) copy-start(f32[2,6,32,512]{3,2,1,0:T(8,128)} %get-tuple-element.11) | copy-start | bytes 2359300
  233.0 63.8 %all-to-all-start = ((bf16[8,2,98304]{2,1,0:T(2,128)(2,1)}), bf16[8,2,98304]{2,1,0:T(2,128)(2,1)}, u32[]{:S(2)}, u32[]{:S(2)}) async-start(bf16[8,2,98304]{2,1,0:T(2,128)(2,1)} %reshape.250), calls=%async_computation | async-start | bytes 6291456 | tf_op jit(solution)/shard_map/all_to_all | solution.py:135
  243.8 98.7 %all-gather.5.cloned.1.call-start = ((), (), s32[]{:S(2)}) async-start(), calls=%async_computation.2 | async-start | bytes 7077888 | tf_op jit(solution)/shard_map/all_gather | solution.py:133
  245.3 5.1 %copy-start.16 = (s32[48]{0:T(128)S(1)}, s32[48]{0:T(128)}, u32[]{:S(2)}) copy-start(s32[48]{0:T(128)} %param.24) | copy-start | bytes 580
  245.3 5.2 %copy-start.17 = (f32[8]{0:T(128)S(1)}, f32[8]{0:T(128)}, u32[]{:S(2)}) copy-start(f32[8]{0:T(128)} %param.38) | copy-start | bytes 100
  245.3 5.3 %copy-start.3 = (f32[2,6,32,512]{3,2,1,0:T(8,128)S(1)}, f32[2,6,32,512]{3,2,1,0:T(8,128)}, u32[]{:S(2)}) copy-start(f32[2,6,32,512]{3,2,1,0:T(8,128)} %get-tuple-element.10) | copy-start | bytes 2359300
  342.5 10.3 %copy-start.1 = (bf16[8,2,6,32,8,64]{5,4,3,2,0,1:T(8,128)(2,1)S(1)}, bf16[8,2,6,32,8,64]{5,4,3,2,0,1:T(8,128)(2,1)}, u32[]{:S(2)}) copy-start(bf16[8,2,6,32,8,64]{5,4,3,2,0,1:T(8,128)(2,1)} %copy.81) | copy-start | bytes 9437188
  363.5 2.4 copy-start.14
  365.9 4.6 %copy-start.12 = (f32[512]{0:T(512)S(1)}, f32[512]{0:T(512)}, u32[]{:S(2)}) copy-start(f32[512]{0:T(512)} %param.43) | copy-start | bytes 6148
  365.9 4.6 %copy-start.13 = (f32[512]{0:T(512)S(1)}, f32[512]{0:T(512)}, u32[]{:S(2)}) copy-start(f32[512]{0:T(512)} %param.42) | copy-start | bytes 6148
  365.9 5.9 %copy-start.8 = (f32[2,6,32]{2,0,1:T(2,128)S(1)}, f32[2,6,32]{2,0,1:T(2,128)}, u32[]{:S(2)}) copy-start(f32[2,6,32]{2,0,1:T(2,128)} %param.22) | copy-start | bytes 4612
Sparse Core Ops, SparseCore 0:
  13.7 96.4 all-gather.2
  250.4 92.0 all-gather.4
